TPU v7x, 32 devices: a whole 2x2x4 slice. The times are simulated.
32 devices in a mesh: copies: 2 (over x), expert: 4 (over y, core), tm: 4 (over z).
Axes of the slice: x: 2, y: 2, z: 4, core: 2. Of those that a mesh axis runs over, the one named last changes fastest.
Arguments:
- tokens: bfloat16 [4, 1024, 2048], P('tm', ('copies', 'expert')), parts along dimension 1, may hold values from -6 to 6
- route_ids: int32 [4, 1024, 6], P('tm', ('copies', 'expert')), parts along dimension 1, may hold values from 0 to 15, all different within a row; in each aligned block of 128 rows (0 to 127, 128 to 255, ..., all dimensions but the last counted through in order) at most 72 rows name the same one
- route_probs: float32 [4, 1024, 6], P('tm', ('copies', 'expert')), parts along dimension 1, may hold values from 0.05 to 1
- step_size: float32 [8], P(('copies', 'tm')), parts along dimension 0, may hold values from 0.2 to 0.6
- start_state: float32 [1024, 2048], P(('copies', 'expert')), parts along dimension 0, may hold values from -6 to 6
- w_gate: bfloat16 [16, 2048, 768], P('expert'), may hold values from -0.125 to 0.125
- w_up: bfloat16 [16, 2048, 768], P('expert'), may hold values from -0.125 to 0.125
- w_down: bfloat16 [16, 768, 2048], P('expert'), may hold values from -0.21875 to 0.21875
Outputs:
- new_iterate: float32 [4, 1024, 2048], P('tm', ('copies', 'expert')), parts along dimension 1
There are 2 independent parts, one for each index of `copies`. A program takes and returns all parts, laid end to end along the dimension named above; an argument that names none is the same for every part. Nothing has to cross between parts.
Inputs may be any that keep to these rules, and one draw needn't show every extreme that they name: `route_ids`: each row names 6 different experts. In each aligned block of 128 rows (the tokens of one device), no expert is named by more than 72 rows, a bound that some block reaches.
All inputs are finite; a program needn't handle non-finite values.
Results may differ from a plain program's by a relative error of at most 0.0018.
Values may be sent and summed in bfloat16 or wider, within the bound.
A program may use at most 128 MiB of HBM per device.

v0:
```python
import jax
import jax.numpy as jnp
from jax import lax
from jax.sharding import PartitionSpec as P


def expert_rows(received, w_gate, w_up, w_down):
    local_count, source_count, slot_count, feature_count = received.shape
    flat_rows = received.reshape(local_count, source_count * slot_count, feature_count)
    gate_act = jnp.einsum("jrd,jdf->jrf", flat_rows, w_gate, preferred_element_type=jnp.float32)
    up_act = jnp.einsum("jrd,jdf->jrf", flat_rows, w_up, preferred_element_type=jnp.float32)
    hidden = (jax.nn.silu(gate_act) * up_act).astype(jnp.bfloat16)
    result = jnp.einsum("jrf,jfd->jrd", hidden, w_down, preferred_element_type=jnp.float32)
    return result.astype(jnp.bfloat16).reshape(local_count, source_count, slot_count, feature_count)


def shards(tokens, route_ids, route_probs, step_size, start_state, w_gate, w_up, w_down):
    tok_count = tokens.shape[1]
    feature_count = tokens.shape[2]
    topk_count = route_ids.shape[2]
    expert_total = w_gate.shape[0] * lax.axis_size("expert")
    capacity = 3 * tok_count * topk_count // (2 * expert_total)
    values = tokens[0].astype(jnp.float32)
    normed = (values * lax.rsqrt(jnp.mean(values * values, axis=-1, keepdims=True) + 1e-06)).astype(
        jnp.bfloat16
    )
    flat_ids = route_ids[0].reshape(-1)
    one_hot = (flat_ids[:, None] == jnp.arange(expert_total, dtype=jnp.int32)[None, :]).astype(
        jnp.int32
    )
    earlier = jnp.cumsum(one_hot, axis=0) - one_hot
    position = jnp.sum(earlier * one_hot, axis=1)
    slot_index = flat_ids * capacity + position
    slot_grid = slot_index[:, None] == jnp.arange(expert_total * capacity, dtype=jnp.int32)[None, :]
    dispatch_map = jnp.any(slot_grid.reshape(tok_count, topk_count, -1), axis=1).astype(
        jnp.bfloat16
    )
    packed = jnp.einsum(
        "ts,td->sd", dispatch_map, normed, preferred_element_type=jnp.float32
    ).astype(jnp.bfloat16)
    outgoing = packed.reshape(expert_total, 1, capacity, feature_count)
    received = lax.all_to_all(outgoing, "expert", split_axis=0, concat_axis=1, tiled=True)
    answered = expert_rows(received, w_gate, w_up, w_down)
    returned = lax.all_to_all(answered, "expert", split_axis=1, concat_axis=0, tiled=True)
    gathered = returned.reshape(expert_total * capacity, feature_count)[slot_index]
    gathered = gathered.reshape(tok_count, topk_count, feature_count).astype(jnp.float32)
    gate_probs = route_probs[0]
    weights = gate_probs / jnp.sum(gate_probs, axis=-1, keepdims=True)
    drift_rows = jnp.einsum("tk,tkd->td", weights, gathered, precision=lax.Precision.HIGHEST)
    increment = step_size[0] * drift_rows
    own_index = lax.axis_index("tm")
    shard_rows = lax.all_gather(
        increment[None].astype(jnp.bfloat16), "tm", axis=0, tiled=True
    ).astype(jnp.float32)
    below_own = jnp.arange(shard_rows.shape[0], dtype=jnp.int32) <= own_index
    summed = jnp.zeros_like(increment) + jnp.sum(
        jnp.where(below_own[:, None, None], shard_rows, 0.0), axis=0
    )
    return (start_state + summed)[None]


def solution(mesh):
    return jax.shard_map(
        shards,
        mesh=mesh,
        in_specs=(
            P("tm", ("copies", "expert"), None),
            P("tm", ("copies", "expert"), None),
            P("tm", ("copies", "expert"), None),
            P(("copies", "tm")),
            P(("copies", "expert"), None),
            P("expert", None, None),
            P("expert", None, None),
            P("expert", None, None),
        ),
        out_specs=P("tm", ("copies", "expert"), None),
        check_vma=False,
    )
```

profile of v0, /device:TPU:0, one launch (start us, length us, event | category | flops | bytes accessed | tf_op | source)
XLA Modules:
  0.0 237.0 jit_solution(10654996169284588786)
XLA Ops:
  6.5 0.8 copy.25
  7.3 0.1 eq.43
  7.5 0.1 eq.39
  7.6 1.7 reduce-window.6
  9.3 0.3 slice_reduce_fusion
  9.6 0.1 fusion.11
  9.7 0.1 reduce_sum.42
  9.9 0.1 copy.29
  9.9 0.6 fusion.1
  10.5 1.2 fusion.3
  11.8 2.7 %convolution_convert_fusion = bf16[1152,2048]{1,0:T(8,128)(2,1)S(1)} fusion(pred[128,1152]{1,0:T(8,128)(4,1)S(1)} %fusion.1, bf16[1,128,2048]{2,1,0:T(8,128)(2,1)} %param.8, f32[128]{0:T(128)S(1)} %add_rsqrt_fusion), kind=kOutput, calls=%fused_computation.1 | convolution fusion | flops 607125504 | bytes 5390848 | tf_op jit(solution)/shard_map/ts,td->sd/dot_general | solution.py:38
  14.4 0.0 slice-start.1
  14.5 58.1 %all_to_all.30 = bf16[16,1,72,2048]{3,2,1,0:T(8,128)(2,1)S(1)} all-to-all(bf16[16,1,72,2048]{3,2,1,0:T(8,128)(2,1)S(1)} %bitcast.66), channel_id=1, replica_groups=mesh['copies'=2,'expert'=4,'tm'=4] {'expert'}, dimensions={0} | all-to-all | bytes 9437184 | tf_op jit(solution)/shard_map/all_to_all | solution.py:42
  72.5 0.7 copy.31
  73.3 2.2 copy-done
  75.5 0.6 slice-done.2
  76.0 5.7 %fusion.16 = f32[4,288,768]{2,1,0:T(8,128)} fusion(bf16[4,288,2048]{2,1,0:T(8,128)(2,1)S(1)} %bitcast.68, bf16[4,2048,768]{2,1,0:T(8,128)(2,1)S(1)} %bitcast.74), kind=kOutput, calls=%fused_computation.37 | convolution fusion | flops 3623878656 | bytes 20840448 | tf_op jit(solution)/shard_map/jrd,jdf->jrf/dot_general | solution.py:10
  81.7 15.9 %convolution_convert_fusion.1 = bf16[4,288,2048]{2,1,0:T(8,128)(2,1)} fusion(bf16[4,768,2048]{2,1,0:T(8,128)(2,1)} %param.15, f32[4,288,768]{2,1,0:T(8,128)} %fusion.16, bf16[4,288,2048]{2,1,0:T(8,128)(2,1)} %bitcast.69, bf16[4,2048,768]{2,1,0:T(8,128)(2,1)} %param.14), kind=kOutput, calls=%fused_computation.4 | convolution fusion | flops 7255425024 | bytes 38141952 | tf_op jit(solution)/shard_map/jrf,jfd->jrd/dot_general | solution.py:13
  97.6 5.2 %copy.32 = bf16[4,4,72,2048]{3,2,0,1:T(8,128)(2,1)} copy(bf16[4,4,72,2048]{3,2,1,0:T(8,128)(2,1)} %bitcast.70) | data formatting | bytes 9437184 | tf_op jit(solution)/shard_map/reshape | solution.py:14
  102.8 5.1 %all-to-all-start.1 = ((bf16[4,4,72,2048]{3,2,0,1:T(8,128)(2,1)}), bf16[4,4,72,2048]{3,2,0,1:T(8,128)(2,1)}, u32[]{:S(2)}, u32[]{:S(2)}) async-start(bf16[4,4,72,2048]{3,2,0,1:T(8,128)(2,1)} %copy.32), calls=%async_computation.1 | async-start | bytes 9437184 | tf_op jit(solution)/shard_map/all_to_all | solution.py:44
  107.9 0.2 all-gather.3.cloned.1.call-start
  108.1 0.1 mul.59
  108.3 0.1 copy.33
  109.1 52.6 %all-to-all-done.1 = bf16[4,4,72,2048]{3,2,0,1:T(8,128)(2,1)} async-done(((bf16[4,4,72,2048]{3,2,0,1:T(8,128)(2,1)}), bf16[4,4,72,2048]{3,2,0,1:T(8,128)(2,1)}, u32[]{:S(2)}, u32[]{:S(2)}) %all-to-all-start.1) | async-done | bytes 4718624 | tf_op jit(solution)/shard_map/all_to_all | solution.py:44
  161.7 9.3 %gather_fusion = bf16[768,2048]{1,0:T(8,128)(2,1)S(1)} fusion(bf16[1152,2048]{1,0:T(8,128)(2,1)} %bitcast.15, s32[1024]{0:T(1024)S(1)} %pad_clamp_fusion), kind=kCustom, calls=%fused_computation | custom fusion | bytes 6294528 | tf_op jit(solution)/shard_map/gather | solution.py:45
  171.0 2.9 %reshape.100 = bf16[128,6,2048]{2,1,0:T(8,128)(2,1)} reshape(bf16[768,2048]{1,0:T(8,128)(2,1)S(1)} %gather_fusion) | data formatting | bytes 6291456 | tf_op jit(solution)/shard_map/reshape | solution.py:46
  173.8 5.7 %fusion.17 = f32[128,1,2048]{2,1,0:T(1,128)S(1)} fusion(f32[128,6,1]{1,2,0:T(1,128)S(1)} %copy.33, bf16[128,6,2048]{2,1,0:T(8,128)(2,1)} %reshape.100), kind=kOutput, calls=%fused_computation.38 | convolution fusion | flops 18874368 | bytes 4197376 | tf_op jit(solution)/shard_map/tk,tkd->td/dot_general | solution.py:49
  179.6 1.1 fusion.5
  180.7 0.0 all-gather.3.cloned.1.call-update
  180.7 46.1 %all-gather.3.cloned.1.call-done = bf16[512,2048]{1,0:T(8,128)(2,1)} async-done(((bf16[128,2048]{1,0:T(8,128)(2,1)}), bf16[512,2048]{1,0:T(8,128)(2,1)}) %all-gather.3.cloned.1.call-update) | async-done | bytes 2097168 | tf_op jit(solution)/shard_map/all_gather | solution.py:52
  226.8 2.2 fusion
  229.0 1.1 add_bitcast_fusion
  (20 shorter events, 0.1 us)
Async XLA Ops:
  11.8 63.7 %slice-start = ((s8[12582912]{0:T(1024)(128)(4,1)}), s8[4194304]{0:T(1024)(128)(4,1)S(1)}, s32[]{:S(2)}) async-start(s8[12582912]{0:T(1024)(128)(4,1)} %bitcast.73), calls=%async_computation.3 | async-start | bytes 8388608
  14.4 61.0 %slice-start.1 = ((s8[12582912]{0:T(1024)(128)(4,1)}), s8[4194304]{0:T(1024)(128)(4,1)S(1)}, s32[]{:S(2)}) async-start(s8[12582912]{0:T(1024)(128)(4,1)} %bitcast.73), calls=%async_computation.4 | async-start | bytes 8388608
  72.5 3.5 %slice-start.2 = ((s8[12582912]{0:T(1024)(128)(4,1)}), s8[4194304]{0:T(1024)(128)(4,1)S(1)}, s32[]{:S(2)}) async-start(s8[12582912]{0:T(1024)(128)(4,1)} %bitcast.73), calls=%async_computation.5 | async-start | bytes 8388608
  73.3 2.2 copy-start
  102.8 5.5 %copy-start.2 = (f32[1,128,6]{1,0,2:T(1,128)S(1)}, f32[1,128,6]{1,0,2:T(1,128)}, u32[]{:S(2)}) copy-start(f32[1,128,6]{1,0,2:T(1,128)} %param.10) | copy-start | bytes 9220
  102.8 58.9 %all-to-all-start.1 = ((bf16[4,4,72,2048]{3,2,0,1:T(8,128)(2,1)}), bf16[4,4,72,2048]{3,2,0,1:T(8,128)(2,1)}, u32[]{:S(2)}, u32[]{:S(2)}) async-start(bf16[4,4,72,2048]{3,2,0,1:T(8,128)(2,1)} %copy.32), calls=%async_computation.1 | async-start | bytes 9437184 | tf_op jit(solution)/shard_map/all_to_all | solution.py:44
  107.9 118.9 %all-gather.3.cloned.1.call-start = ((), (), s32[]{:S(2)}) async-start(), calls=%async_computation.2 | async-start | bytes 2621440 | tf_op jit(solution)/shard_map/all_gather | solution.py:52
  173.8 55.2 %copy-start.1 = (f32[128,2048]{1,0:T(8,128)S(1)}, f32[128,2048]{1,0:T(8,128)}, u32[]{:S(2)}) copy-start(f32[128,2048]{1,0:T(8,128)} %param.12) | copy-start | bytes 3145732
Sparse Core Ops, SparseCore 0:
  180.8 45.9 all-gather.2
where the time goes:
time: 237 us
  waiting for transfers between devices  98.7 us (42%)
  blocking collectives  58.1 us (25%)
  matrix products  29.9 us (13%)
  local copies, waits for them, and re-layouts  22.6 us (10%)
  between operations  14.2 us (6%)
  other arithmetic  8.19 us (3%)
  starting transfers between devices  5.28 us (2%)
    all_to_all x1, blocking collectives, shards(): lax.all_to_all(outgoing, 'expert', split_axis=0, concat_axis=1, tiled=True)  58.1 us
    all_to_all x1, waiting for transfers between devices, shards(): lax.all_to_all(answered, 'expert', split_axis=1, concat_axis=0, tiled=True)  52.6 us
    all_gather x1, waiting for transfers between devices, shards(): lax.all_gather(increment[None].astype(jnp.bfloat16), 'tm', axis=0, tiled=...  46.1 us
    dot_general x1, matrix products, expert_rows(): jnp.einsum('jrf,jfd->jrd', hidden, w_down, preferred_element_type=jnp.flo...  15.9 us
    gather x1, local copies, waits for them, and re-layouts, shards(): returned.reshape(expert_total * capacity, feature_count)[slot_index]  9.28 us
    dot_general x1, matrix products, shards(): jnp.einsum('tk,tkd->td', weights, gathered, precision=lax.Precision.HIGHEST)  5.74 us
    dot_general x1, matrix products, expert_rows(): jnp.einsum('jrd,jdf->jrf', flat_rows, w_gate, preferred_element_type=jnp....  5.66 us
    reshape x1, local copies, waits for them, and re-layouts, expert_rows(): result.astype(jnp.bfloat16)  5.23 us
  transfers between devices with their start and end apart: 2, of which 2 were waited for; matrix products, arithmetic and copies ran while one was open for 0% of the time, Pallas kernels for 0%

commit v1 on v0

--- a/solution.py
+++ b/solution.py
@@ -41,7 +41,18 @@
     outgoing = packed.reshape(expert_total, 1, capacity, feature_count)
     received = lax.all_to_all(outgoing, "expert", split_axis=0, concat_axis=1, tiled=True)
     answered = expert_rows(received, w_gate, w_up, w_down)
-    returned = lax.all_to_all(answered, "expert", split_axis=1, concat_axis=0, tiled=True)
+    ways, here = (lax.axis_size("expert"), lax.axis_index("expert"))
+    width = answered.shape[1] // ways
+    shape = list(answered.shape)
+    shape[1] = width
+    height = shape[0]
+    shape[0] = height * ways
+    returned = jnp.zeros(shape, answered.dtype)
+    for mask in range(ways):
+        part = lax.dynamic_slice_in_dim(answered, (here ^ mask) * width, width, axis=1)
+        if mask:
+            part = lax.ppermute(part, "expert", [(d, d ^ mask) for d in range(ways)])
+        returned = lax.dynamic_update_slice_in_dim(returned, part, (here ^ mask) * height, axis=0)
     gathered = returned.reshape(expert_total * capacity, feature_count)[slot_index]
     gathered = gathered.reshape(tok_count, topk_count, feature_count).astype(jnp.float32)
     gate_probs = route_probs[0]

time: 237 us -> 241 us (1.017)
  blocking collectives: 58.1 us -> 0 us
  waiting for transfers between devices: 98.7 us -> 144 us
  local copies, waits for them, and re-layouts: 22.6 us -> 31.6 us
  matrix products: 29.9 us -> 34.9 us
    all_to_all x1 -> x0, blocking collectives: 58.1 us -> none  [shards(): lax.all_to_all(outgoing, 'expert', split_axis=0, concat_axis=1, tiled=True)]
    ppermute x0 -> x3, waiting for transfers between devices: none -> 43.2 us  [shards(): part = lax.ppermute(part, 'expert', [(d, d ^ mask) for d in range(ways)])]
    dynamic_update_slice x0 -> x4, local copies, waits for them, and re-layouts: none -> 5.88 us  [shards(): lax.dynamic_update_slice_in_dim(returned, part, (here ^ mask) * height, a...]
    reshape x1 -> x0, local copies, waits for them, and re-layouts: 5.23 us -> none  [expert_rows(): result.astype(jnp.bfloat16)]
    dynamic_slice x0 -> x1, local copies, waits for them, and re-layouts: none -> 3.9 us  [shards(): lax.dynamic_slice_in_dim(answered, (here ^ mask) * width, width, axis=1)]
    dot_general x1, matrix products: 5.66 us -> 8.58 us  [expert_rows(): jnp.einsum('jrd,jdf->jrf', flat_rows, w_gate, preferred_element_type=jnp....]
    broadcast_in_dim x0 -> x1, local copies, waits for them, and re-layouts: none -> 2.76 us  [shards(): returned = jnp.zeros(shape, answered.dtype)]
  transfers between devices with their start and end apart: 2 -> 5, of which waited for: 2 -> 4; matrix products, arithmetic and copies ran while one was open for 0% -> 3% of each run, Pallas kernels for 0% -> 0%
where the time goes in v1:
time: 241 us; the launch traced here: 240 us
  waiting for transfers between devices  144 us (60%)
  matrix products  34.9 us (14%)
  local copies, waits for them, and re-layouts  31.6 us (13%)
  between operations  14.3 us (6%)
  other arithmetic  8.19 us (3%)
  starting transfers between devices  7.13 us (3%)
    all_to_all x1, waiting for transfers between devices, shards(): lax.all_to_all(outgoing, 'expert', split_axis=0, concat_axis=1, tiled=True)  54.2 us
    all_gather x1, waiting for transfers between devices, shards(): lax.all_gather(increment[None].astype(jnp.bfloat16), 'tm', axis=0, tiled=...  46.9 us
    ppermute x3, waiting for transfers between devices, shards(): part = lax.ppermute(part, 'expert', [(d, d ^ mask) for d in range(ways)])  43.2 us
    dot_general x1, matrix products, expert_rows(): jnp.einsum('jrf,jfd->jrd', hidden, w_down, preferred_element_type=jnp.flo...  15.9 us
    gather x1, local copies, waits for them, and re-layouts, shards(): returned.reshape(expert_total * capacity, feature_count)[slot_index]  9.28 us
    dot_general x1, matrix products, expert_rows(): jnp.einsum('jrd,jdf->jrf', flat_rows, w_gate, preferred_element_type=jnp....  8.58 us
    dynamic_update_slice x4, local copies, waits for them, and re-layouts, shards(): lax.dynamic_update_slice_in_dim(returned, part, (here ^ mask) * height, a...  5.88 us
    dot_general x1, matrix products, shards(): jnp.einsum('tk,tkd->td', weights, gathered, precision=lax.Precision.HIGHEST)  5.74 us
  transfers between devices with their start and end apart: 5, of which 4 were waited for; matrix products, arithmetic and copies ran while one was open for 3% of the time, Pallas kernels for 0%

profile of v1, /device:TPU:0, one launch (start us, length us, event | category | flops | bytes accessed | tf_op | source)
XLA Modules:
  0.0 240.5 jit_solution(17294049575246311470)
XLA Ops:
  6.5 0.8 copy.34
  7.3 0.1 eq.43
  7.5 0.1 eq.39
  7.6 1.7 reduce-window.6
  9.3 0.3 slice_reduce_fusion
  9.9 0.6 fusion.1
  10.5 1.2 fusion.3
  11.8 4.7 %convolution_convert_fusion = bf16[1152,2048]{1,0:T(8,128)(2,1)} fusion(pred[128,1152]{1,0:T(8,128)(4,1)S(1)} %fusion.1, bf16[1,128,2048]{2,1,0:T(8,128)(2,1)} %param.8, f32[128]{0:T(128)S(1)} %add_rsqrt_fusion), kind=kOutput, calls=%fused_computation.1 | convolution fusion | flops 607125504 | bytes 5390848 | tf_op jit(solution)/shard_map/ts,td->sd/dot_general | solution.py:38
  16.5 4.9 %all-to-all-start = ((bf16[16,1,72,2048]{3,2,1,0:T(8,128)(2,1)}), bf16[16,1,72,2048]{3,2,1,0:T(8,128)(2,1)}, u32[]{:S(2)}, u32[]{:S(2)}) async-start(bf16[16,1,72,2048]{3,2,1,0:T(8,128)(2,1)} %bitcast.70), calls=%async_computation | async-start | bytes 9437184 | tf_op jit(solution)/shard_map/all_to_all | solution.py:42
  21.4 0.2 all-gather.3.cloned.1.call-start
  21.7 54.2 %all-to-all-done = bf16[16,1,72,2048]{3,2,1,0:T(8,128)(2,1)} async-done(((bf16[16,1,72,2048]{3,2,1,0:T(8,128)(2,1)}), bf16[16,1,72,2048]{3,2,1,0:T(8,128)(2,1)}, u32[]{:S(2)}, u32[]{:S(2)}) %all-to-all-start) | async-done | bytes 4718624 | tf_op jit(solution)/shard_map/all_to_all | solution.py:42
  75.9 3.0 %copy.40 = bf16[4,4,1,72,2048]{4,3,0,1,2:T(8,128)(2,1)S(1)} copy(bf16[4,4,1,72,2048]{4,3,1,0,2:T(8,128)(2,1)} %bitcast.8) | data formatting | bytes 9437184 | tf_op jit(solution)/shard_map/all_to_all | solution.py:42
  79.0 2.2 copy-done
  81.1 8.6 %fusion.16 = f32[4,288,768]{2,1,0:T(8,128)} fusion(bf16[4,288,2048]{2,1,0:T(8,128)(2,1)S(1)} %bitcast.71, bf16[4,2048,768]{2,1,0:T(8,128)(2,1)} %param.13), kind=kOutput, calls=%fused_computation.44 | convolution fusion | flops 3623878656 | bytes 20840448 | tf_op jit(solution)/shard_map/jrd,jdf->jrf/dot_general | solution.py:10
  89.7 15.9 %convolution_convert_fusion.1 = bf16[4,288,2048]{2,1,0:T(8,128)(2,1)} fusion(bf16[4,768,2048]{2,1,0:T(8,128)(2,1)} %param.15, f32[4,288,768]{2,1,0:T(8,128)} %fusion.16, bf16[4,288,2048]{2,1,0:T(8,128)(2,1)} %bitcast.72, bf16[4,2048,768]{2,1,0:T(8,128)(2,1)} %param.14), kind=kOutput, calls=%fused_computation.4 | convolution fusion | flops 7255425024 | bytes 38141952 | tf_op jit(solution)/shard_map/jrf,jfd->jrd/dot_general | solution.py:13
  105.6 3.9 %constant_dynamic-slice_fusion = (bf16[4,1,72,2048]{3,2,1,0:T(8,128)(2,1)}, bf16[4,1,72,2048]{3,2,1,0:T(8,128)(2,1)}, bf16[4,1,72,2048]{3,2,1,0:T(8,128)(2,1)}) fusion(bf16[4,4,72,2048]{3,2,1,0:T(8,128)(2,1)} %bitcast.73, s32[]{:T(128)S(6)} %select_n.44, s32[]{:T(128)S(6)} %select_n.42, s32[]{:T(128)S(6)} %select_n.40), kind=kLoop, calls=%fused_computation.38 | loop fusion | bytes 7077900 | tf_op jit(solution)/shard_map/dynamic_slice | solution.py:52
  109.5 0.1 mul.75
  110.6 1.9 collective-permute-start.2
  112.5 2.8 %broadcast_in_dim.17 = bf16[16,1,72,2048]{3,2,0,1:T(8,128)(2,1)} broadcast(bf16[]{:T(256)} %constant.18.clone.1), dimensions={} | broadcast | bytes 4718594 | tf_op jit(solution)/shard_map/broadcast_in_dim | solution.py:50
  115.2 2.5 %bitcast_dynamic-update-slice_fusion.3 = bf16[16,1,72,2048]{3,2,0,1:T(8,128)(2,1)} fusion(bf16[16,1,72,2048]{3,2,0,1:T(8,128)(2,1)} %broadcast_in_dim.17, s32[]{:T(128)S(6)} %select_n.39, bf16[4,4,72,2048]{3,2,1,0:T(8,128)(2,1)} %bitcast.74, s32[]{:T(128)S(6)} %select_n.38), kind=kLoop, calls=%fused_computation.14 | loop fusion | bytes 2359304 | tf_op jit(solution)/shard_map/dynamic_update_slice | solution.py:55
  117.7 1.1 bitcast_dynamic-update-slice_fusion.2
  118.8 20.0 %collective-permute-done.1 = bf16[4,1,72,2048]{3,2,1,0:T(8,128)(2,1)S(1)} collective-permute-done((bf16[4,1,72,2048]{3,2,1,0:T(8,128)(2,1)}, bf16[4,1,72,2048]{3,2,1,0:T(8,128)(2,1)S(1)}, u32[]{:S(2)}, u32[]{:S(2)}) %collective-permute-start.1) | collective-permute-done | bytes 1179680 | tf_op jit(solution)/shard_map/ppermute | solution.py:54
  138.8 1.1 bitcast_dynamic-update-slice_fusion.1
  139.9 23.3 %collective-permute-done.2 = bf16[4,1,72,2048]{3,2,1,0:T(8,128)(2,1)S(1)} collective-permute-done((bf16[4,1,72,2048]{3,2,1,0:T(8,128)(2,1)}, bf16[4,1,72,2048]{3,2,1,0:T(8,128)(2,1)S(1)}, u32[]{:S(2)}, u32[]{:S(2)}) %collective-permute-start.2) | collective-permute-done | bytes 1179680 | tf_op jit(solution)/shard_map/ppermute | solution.py:54
  163.1 1.2 bitcast_dynamic-update-slice_fusion
  164.4 9.3 %gather_fusion = bf16[768,2048]{1,0:T(8,128)(2,1)S(1)} fusion(bf16[1152,2048]{1,0:T(8,128)(2,1)} %bitcast.17, s32[1024]{0:T(1024)S(1)} %pad_clamp_fusion), kind=kCustom, calls=%fused_computation | custom fusion | bytes 6294528 | tf_op jit(solution)/shard_map/gather | solution.py:56
  173.7 2.9 %reshape.99 = bf16[128,6,2048]{2,1,0:T(8,128)(2,1)} reshape(bf16[768,2048]{1,0:T(8,128)(2,1)S(1)} %gather_fusion) | data formatting | bytes 6291456 | tf_op jit(solution)/shard_map/reshape | solution.py:57
  176.5 5.7 %fusion.17 = f32[128,1,2048]{2,1,0:T(1,128)S(1)} fusion(f32[128,6,1]{1,2,0:T(1,128)S(1)} %copy.45, bf16[128,6,2048]{2,1,0:T(8,128)(2,1)} %reshape.99), kind=kOutput, calls=%fused_computation.45 | convolution fusion | flops 18874368 | bytes 4197376 | tf_op jit(solution)/shard_map/tk,tkd->td/dot_general | solution.py:60
  182.3 1.1 fusion.5
  183.4 46.9 %all-gather.3.cloned.1.call-done = bf16[512,2048]{1,0:T(8,128)(2,1)} async-done(((bf16[128,2048]{1,0:T(8,128)(2,1)}), bf16[512,2048]{1,0:T(8,128)(2,1)}) %all-gather.3.cloned.1.call-update) | async-done | bytes 2097168 | tf_op jit(solution)/shard_map/all_gather | solution.py:63
  230.3 2.2 fusion
  232.5 1.1 add_bitcast_fusion
  (23 shorter events, 0.6 us)
Async XLA Ops:
  16.5 59.4 %all-to-all-start = ((bf16[16,1,72,2048]{3,2,1,0:T(8,128)(2,1)}), bf16[16,1,72,2048]{3,2,1,0:T(8,128)(2,1)}, u32[]{:S(2)}, u32[]{:S(2)}) async-start(bf16[16,1,72,2048]{3,2,1,0:T(8,128)(2,1)} %bitcast.70), calls=%async_computation | async-start | bytes 9437184 | tf_op jit(solution)/shard_map/all_to_all | solution.py:42
  21.4 208.9 %all-gather.3.cloned.1.call-start = ((), (), s32[]{:S(2)}) async-start(), calls=%async_computation.1 | async-start | bytes 2621440 | tf_op jit(solution)/shard_map/all_gather | solution.py:63
  78.9 2.2 copy-start
  105.6 4.1 %copy-start.2 = (f32[1,128,6]{1,0,2:T(1,128)S(1)}, f32[1,128,6]{1,0,2:T(1,128)}, u32[]{:S(2)}) copy-start(f32[1,128,6]{1,0,2:T(1,128)} %param.10) | copy-start | bytes 9220
  109.5 8.2 %collective-permute-start = (bf16[4,1,72,2048]{3,2,1,0:T(8,128)(2,1)}, bf16[4,1,72,2048]{3,2,1,0:T(8,128)(2,1)S(1)}, u32[]{:S(2)}, u32[]{:S(2)}) collective-permute-start(bf16[4,1,72,2048]{3,2,1,0:T(8,128)(2,1)} %get-tuple-element.7), channel_id=1, source_target_pairs={{0,4},{4,0},{8,12},{12,8},{1,5},{5,1},{9,13},{13,9},{2,6},{6,2},{1... | collective-permute-start | bytes 3538952 | tf_op jit(solution)/shard_map/ppermute | solution.py:54
  109.7 29.1 %collective-permute-start.1 = (bf16[4,1,72,2048]{3,2,1,0:T(8,128)(2,1)}, bf16[4,1,72,2048]{3,2,1,0:T(8,128)(2,1)S(1)}, u32[]{:S(2)}, u32[]{:S(2)}) collective-permute-start(bf16[4,1,72,2048]{3,2,1,0:T(8,128)(2,1)} %get-tuple-element.6), channel_id=1, source_target_pairs={{0,8},{4,12},{8,0},{12,4},{1,9},{5,13},{9,1},{13,5},{2,10},{6,14},... | collective-permute-start | bytes 3538952 | tf_op jit(solution)/shard_map/ppermute | solution.py:54
  110.6 52.6 %collective-permute-start.2 = (bf16[4,1,72,2048]{3,2,1,0:T(8,128)(2,1)}, bf16[4,1,72,2048]{3,2,1,0:T(8,128)(2,1)S(1)}, u32[]{:S(2)}, u32[]{:S(2)}) collective-permute-start(bf16[4,1,72,2048]{3,2,1,0:T(8,128)(2,1)} %get-tuple-element.5), channel_id=1, source_target_pairs={{0,12},{4,8},{8,4},{12,0},{1,13},{5,9},{9,5},{13,1},{2,14},{6,10},... | collective-permute-start | bytes 3538952 | tf_op jit(solution)/shard_map/ppermute | solution.py:54
  176.5 56.0 %copy-start.1 = (f32[128,2048]{1,0:T(8,128)S(1)}, f32[128,2048]{1,0:T(8,128)}, u32[]{:S(2)}) copy-start(f32[128,2048]{1,0:T(8,128)} %param.12) | copy-start | bytes 3145732
Sparse Core Ops, SparseCore 0:
  183.5 46.7 all-gather.2
